TPU v7x, 512 devices: a whole 4x4x16 slice. The times are simulated.
512 devices in a mesh: group: 16 (over x, y), dev: 32 (over z, core).
Axes of the slice: x: 4, y: 4, z: 16, core: 2. Of those that a mesh axis runs over, the one named last changes fastest.
Arguments:
- embeddings: bfloat16 [655360, 768], P(('group', 'dev')), may hold values from -6 to 6
- projection: bfloat16 [256, 768], replicated, may hold values from -0.21875 to 0.21875
- triplets: int32 [3, 1048576], P(None, ('group', 'dev')), may hold values from 0 to 3327, as said below
- cotangent: float32 [1048576], P(('group', 'dev')), may hold values from -24 to 24
- wanted_rows: int32 [8192, 128], P(('group', 'dev')), may hold values from -1 to 1279, as said below
Outputs:
- row_grad: bfloat16 [655360, 768], P(('group', 'dev'))
- weight_grad: float32 [256, 768], replicated
Inputs may be any that keep to these rules, and one draw needn't show every extreme that they name: `wanted_rows`: in each list the live entries come first and are distinct rows of the owning device, the rest are -1; each list holds from 128 // 4 (at least 1) to 128 live entries; all lists of some group of requesters are full, and all lists sent to some group are full. `triplets`: anchors are below 1280; a positive or negative below 1280 is one of the device's own rows, else 1280 + h * 128 + s names a live slot s of the device's list for group h.
All inputs are finite; a program needn't handle non-finite values.
Results may differ from a plain program's by a relative error of at most 0.0058.
Values may be sent and summed in bfloat16 or wider, within the bound.
No kernel may reach another device: no remote copies, remote signals or barrier semaphores. Data moves between devices by JAX's collectives and lax.ppermute only.
A program may use at most 64 MiB of HBM per device.

v0:
```python
import math
import jax
import jax.numpy as jnp
from jax import lax
from jax.sharding import PartitionSpec as P

distance_scale = 0.0625
margin = 1.0
pull_share = 0.5


def triplet_gradients(lookup, triple, cotangent):
    anchor_rows = lookup[triple[0]].astype(jnp.float32)
    positive_rows = lookup[triple[1]].astype(jnp.float32)
    negative_rows = lookup[triple[2]].astype(jnp.float32)
    to_positive = anchor_rows - positive_rows
    to_negative = anchor_rows - negative_rows
    near = distance_scale * jnp.sum(to_positive * to_positive, axis=1)
    far = distance_scale * jnp.sum(to_negative * to_negative, axis=1)
    hinge_gate = jax.nn.sigmoid(margin + near - far)
    pull_factor = 2.0 * distance_scale * cotangent * (1.0 - pull_share + pull_share * hinge_gate)
    push_factor = 2.0 * distance_scale * cotangent * pull_share * hinge_gate
    pull_term = pull_factor[:, None] * to_positive
    push_term = push_factor[:, None] * to_negative
    gradient = jnp.zeros(lookup.shape, jnp.float32)
    gradient = gradient.at[triple[0]].add(pull_term - push_term)
    gradient = gradient.at[triple[1]].add(-pull_term)
    gradient = gradient.at[triple[2]].add(push_term)
    return gradient


def local(embeddings, projection, triplets, cotangent, wanted_rows):
    shard_rows = embeddings.shape[0]
    rank_width = projection.shape[0]
    groups = lax.axis_size("group")
    contract = (((1,), (1,)), ((), ()))
    own_projected = lax.dot_general(
        embeddings, projection, contract, preferred_element_type=jnp.float32
    ).astype(jnp.bfloat16)
    wanted = lax.all_to_all(wanted_rows, "group", split_axis=0, concat_axis=0, tiled=True)
    served_index = jnp.maximum(wanted, 0)
    served = own_projected[served_index]
    fetched = lax.all_to_all(served, "group", split_axis=0, concat_axis=0, tiled=True)
    lookup = jnp.concatenate([own_projected, fetched.reshape(-1, rank_width)], axis=0)
    gradient = triplet_gradients(lookup, triplets, cotangent)
    remote_grad = gradient[shard_rows:].reshape(groups, -1, rank_width).astype(jnp.bfloat16)
    returned = lax.all_to_all(remote_grad, "group", split_axis=0, concat_axis=0, tiled=True)
    row_total = (
        gradient[:shard_rows]
        .at[served_index.reshape(-1)]
        .add(returned.reshape(-1, rank_width).astype(jnp.float32))
    )
    row_rounded = row_total.astype(jnp.bfloat16)
    row_grad = jnp.dot(row_rounded, projection, preferred_element_type=jnp.float32).astype(
        jnp.bfloat16
    )
    partial_value = lax.dot_general(
        row_rounded, embeddings, (((0,), (0,)), ((), ())), preferred_element_type=jnp.float32
    )
    factor = 1.0 / math.sqrt(cotangent.shape[0] * groups * lax.axis_size("dev"))
    weight_total = lax.psum(partial_value, ("group", "dev"))
    return (row_grad, weight_total * factor)


def solution(mesh):
    return jax.shard_map(
        local,
        mesh=mesh,
        in_specs=(
            P(("group", "dev"), None),
            P(),
            P(None, ("group", "dev")),
            P(("group", "dev")),
            P(("group", "dev"), None),
        ),
        out_specs=(P(("group", "dev"), None), P()),
        check_vma=False,
    )
```

profile of v0, /device:TPU:2, one launch (start us, length us, event | category | flops | bytes accessed | tf_op | source)
XLA Modules:
  0.0 648.8 jit_solution(12373123322807966387)
XLA Ops:
  7.2 0.0 copy-start
  7.2 9.3 %all-to-all-start = ((s32[16,1,128]{2,1,0:T(1,128)}), s32[16,1,128]{2,1,0:T(1,128)S(1)}, u32[]{:S(2)}, u32[]{:S(2)}) async-start(s32[16,1,128]{2,1,0:T(1,128)} %bitcast.29), calls=%async_computation | async-start | bytes 16384 | tf_op jit(solution)/shard_map/all_to_all | solution.py:40
  16.5 0.0 copy-done
  16.5 1.7 convolution_convert_fusion.1
  18.2 4.5 all-to-all-done
  22.7 9.1 %gather_fusion = bf16[2048,256]{1,0:T(8,128)(2,1)} fusion(bf16[1280,256]{1,0:T(8,128)(2,1)S(1)} %convolution_convert_fusion.1, s32[2048]{0:T(1024)S(1)} %broadcast_clamp_fusion.3), kind=kCustom, calls=%fused_computation | custom fusion | bytes 2105344 | tf_op jit(solution)/shard_map/gather | solution.py:42
  31.8 0.0 copy-start.1
  31.8 5.7 all-to-all-start.1
  37.4 0.0 copy-done.1
  37.5 12.2 %all-to-all-done.1 = bf16[16,128,256]{2,1,0:T(8,128)(2,1)} async-done(((bf16[16,128,256]{2,1,0:T(8,128)(2,1)}), bf16[16,128,256]{2,1,0:T(8,128)(2,1)}, u32[]{:S(2)}, u32[]{:S(2)}) %all-to-all-start.1) | async-done | bytes 1048608 | tf_op jit(solution)/shard_map/all_to_all | solution.py:43
  49.7 2.5 pad_maximum_fusion
  52.2 8.3 %gather_fusion.1 = bf16[2048,256]{1,0:T(8,128)(2,1)S(1)} fusion(bf16[3328,256]{1,0:T(8,128)(2,1)} %pad_maximum_fusion, s32[2048]{0:T(1024)S(1)} %broadcast_clamp_fusion.2), kind=kCustom, calls=%fused_computation.1 | custom fusion | bytes 2105344 | tf_op jit(solution)/shard_map/gather | solution.py:13
  60.5 10.1 %gather_fusion.3 = bf16[2048,256]{1,0:T(8,128)(2,1)} fusion(bf16[3328,256]{1,0:T(8,128)(2,1)} %pad_maximum_fusion, s32[2048]{0:T(1024)S(1)} %broadcast_clamp_fusion), kind=kCustom, calls=%fused_computation.3 | custom fusion | bytes 2105344 | tf_op jit(solution)/shard_map/gather | solution.py:15
  70.7 10.1 %gather_fusion.2 = bf16[2048,256]{1,0:T(8,128)(2,1)} fusion(bf16[3328,256]{1,0:T(8,128)(2,1)} %pad_maximum_fusion, s32[2048]{0:T(1024)S(1)} %broadcast_clamp_fusion.1), kind=kCustom, calls=%fused_computation.2 | custom fusion | bytes 2105344 | tf_op jit(solution)/shard_map/gather | solution.py:14
  80.8 0.0 copy-start.2
  80.8 2.5 multiply_reduce_fusion.1
  83.3 0.0 copy-done.2
  83.3 15.1 %scatter_custom_fusion = f32[3328,256]{1,0:T(8,128)} fusion(s32[2048]{0:T(1024)S(1)} %bitcast.28, bf16[2048,256]{1,0:T(8,128)(2,1)} %gather_fusion.3, bf16[2048,256]{1,0:T(8,128)(2,1)S(1)} %gather_fusion.1, bf16[2048,256]{1,0:T(8,128)(2,1)} %gather_fusion.2, f32[]{:T(128)} %constant.8.clone.1, f32[2048]{0:T(1024)S(1)} %get-tuple-element.8, ...), kind=kCustom, calls=%fused_computation.17 | custom fusion | flops 4718592 | bytes 6569988 | tf_op jit(solution)/shard_map/scatter-add | solution.py:26
  98.4 16.7 %scatter_custom_fusion.1 = f32[3328,256]{1,0:T(8,128)} fusion(f32[3328,256]{1,0:T(8,128)} %scatter_custom_fusion, s32[2048]{0:T(1024)S(1)} %bitcast.26, bf16[2048,256]{1,0:T(8,128)(2,1)} %gather_fusion.2, bf16[2048,256]{1,0:T(8,128)(2,1)S(1)} %gather_fusion.1, f32[2048]{0:T(1024)S(1)} %get-tuple-element.7), kind=kCustom, calls=%fused_computation.15 | custom fusion | flops 3145728 | bytes 5513216 | tf_op jit(solution)/shard_map/scatter-add | solution.py:27
  115.1 16.6 %scatter_custom_fusion.2 = f32[3328,256]{1,0:T(8,128)} fusion(f32[3328,256]{1,0:T(8,128)} %scatter_custom_fusion.1, s32[2048]{0:T(1024)S(1)} %bitcast.24, bf16[2048,256]{1,0:T(8,128)(2,1)} %gather_fusion.3, bf16[2048,256]{1,0:T(8,128)(2,1)S(1)} %gather_fusion.1, f32[2048]{0:T(1024)S(1)} %get-tuple-element.8), kind=kCustom, calls=%fused_computation.23 | custom fusion | flops 2621440 | bytes 5513216 | tf_op jit(solution)/shard_map/scatter-add | solution.py:28
  131.7 2.7 slice.38
  134.4 6.3 all-to-all-start.2
  140.7 0.0 all-reduce.2.cloned.1.call-start
  140.8 1.4 slice.32
  142.2 9.6 %all-to-all-done.2 = bf16[16,128,256]{2,1,0:T(8,128)(2,1)} async-done(((bf16[16,128,256]{2,1,0:T(8,128)(2,1)}), bf16[16,128,256]{2,1,0:T(8,128)(2,1)}, u32[]{:S(2)}, u32[]{:S(2)}) %all-to-all-start.2) | async-done | bytes 1048608 | tf_op jit(solution)/shard_map/all_to_all | solution.py:47
  151.7 13.6 %scatter_custom_fusion.3 = f32[1280,256]{1,0:T(8,128)S(1)} fusion(f32[1280,256]{1,0:T(8,128)S(1)} %slice.32, s32[2048]{0:T(1024)S(1)} %bitcast.22, bf16[2048,256]{1,0:T(8,128)(2,1)} %bitcast.12), kind=kCustom, calls=%fused_computation.13 | custom fusion | flops 1048576 | bytes 2359296 | tf_op jit(solution)/shard_map/scatter-add | solution.py:51
  165.3 1.6 fusion.18
  166.9 0.0 all-reduce.2.cloned.1.call-update
  166.9 2.9 convolution_convert_fusion
  169.9 470.0 %all-reduce.2.cloned.1.call-done = f32[256,768]{1,0:T(8,128)} async-done(((f32[256,768]{1,0:T(8,128)}), f32[256,768]{1,0:T(8,128)}) %all-reduce.2.cloned.1.call-update) | async-done | bytes 786448 | tf_op jit(solution)/shard_map/psum | solution.py:61
  639.9 2.1 broadcast_multiply_fusion
  (7 shorter events, 0.1 us)
Async XLA Ops:
  7.2 9.3 %copy-start = (bf16[1280,768]{1,0:T(8,128)(2,1)S(1)}, bf16[1280,768]{1,0:T(8,128)(2,1)}, u32[]{:S(2)}) copy-start(bf16[1280,768]{1,0:T(8,128)(2,1)} %param.5) | copy-start | bytes 5898244
  7.2 15.5 %all-to-all-start = ((s32[16,1,128]{2,1,0:T(1,128)}), s32[16,1,128]{2,1,0:T(1,128)S(1)}, u32[]{:S(2)}, u32[]{:S(2)}) async-start(s32[16,1,128]{2,1,0:T(1,128)} %bitcast.29), calls=%async_computation | async-start | bytes 16384 | tf_op jit(solution)/shard_map/all_to_all | solution.py:40
  31.8 5.7 copy-start.1
  31.8 17.9 %all-to-all-start.1 = ((bf16[16,128,256]{2,1,0:T(8,128)(2,1)}), bf16[16,128,256]{2,1,0:T(8,128)(2,1)}, u32[]{:S(2)}, u32[]{:S(2)}) async-start(bf16[16,128,256]{2,1,0:T(8,128)(2,1)} %bitcast.20), calls=%async_computation.1 | async-start | bytes 2097152 | tf_op jit(solution)/shard_map/all_to_all | solution.py:43
  80.8 2.5 copy-start.2
  134.4 17.3 %all-to-all-start.2 = ((bf16[16,128,256]{2,1,0:T(8,128)(2,1)}), bf16[16,128,256]{2,1,0:T(8,128)(2,1)}, u32[]{:S(2)}, u32[]{:S(2)}) async-start(bf16[16,128,256]{2,1,0:T(8,128)(2,1)} %bitcast.10), calls=%async_computation.2 | async-start | bytes 2097152 | tf_op jit(solution)/shard_map/all_to_all | solution.py:47
  140.7 499.1 %all-reduce.2.cloned.1.call-start = ((), (), s32[]{:S(2)}) async-start(), calls=%async_computation.3 | async-start | bytes 1572864 | tf_op jit(solution)/shard_map/psum | solution.py:61
Sparse Core Ops, SparseCore 0:
  167.0 472.7 all-reduce.1
where the time goes:
time: 650 us; the launch traced here: 649 us
  waiting for transfers between devices  496 us (76%)
  other arithmetic  69.2 us (11%)
  local copies, waits for them, and re-layouts  41.7 us (6%)
  starting transfers between devices  21.3 us (3%)
  between operations  14.1 us (2%)
    psum x1, waiting for transfers between devices, local(): weight_total = lax.psum(partial_value, ('group', 'dev'))  470 us
    scatter-add x1, other arithmetic, triplet_gradients(): gradient = gradient.at[triple[1]].add(-pull_term)  16.7 us
    scatter-add x1, other arithmetic, triplet_gradients(): gradient = gradient.at[triple[2]].add(push_term)  16.6 us
    scatter-add x1, other arithmetic, triplet_gradients(): gradient = gradient.at[triple[0]].add(pull_term - push_term)  15.1 us
    scatter-add x1, other arithmetic, local(): row_total = gradient[:shard_rows].at[served_index.reshape(-1)].add(return...  13.6 us
  transfers between devices with their start and end apart: 4, of which 4 were waited for; matrix products, arithmetic and copies ran while one was open for 1% of the time, Pallas kernels for 0%

commit v1 on v0

--- a/solution.py
+++ b/solution.py
@@ -7,6 +7,14 @@
 distance_scale = 0.0625
 margin = 1.0
 pull_share = 0.5
+
+
+def return_all_the_signs(load):
+    axis_key = "dev"
+    link_axis = "group"
+    for b in (link_axis, axis_key):
+        load = lax.psum(load, b)
+    return load
 
 
 def triplet_gradients(lookup, triple, cotangent):
@@ -58,7 +66,7 @@
         row_rounded, embeddings, (((0,), (0,)), ((), ())), preferred_element_type=jnp.float32
     )
     factor = 1.0 / math.sqrt(cotangent.shape[0] * groups * lax.axis_size("dev"))
-    weight_total = lax.psum(partial_value, ("group", "dev"))
+    weight_total = return_all_the_signs(partial_value)
     return (row_grad, weight_total * factor)
 
 

time: 650 us -> 511 us (0.79)
  the two profiles are of different devices: /device:TPU:2 before, /device:TPU:1 now
where the time goes in v1:
time: 511 us; the launch traced here: 510 us
  waiting for transfers between devices  362 us (71%)
  other arithmetic  69 us (14%)
  local copies, waits for them, and re-layouts  41.7 us (8%)
  starting transfers between devices  16.6 us (3%)
  between operations  14.2 us (3%)
  matrix products  6.24 us (1%)
    psum x2, waiting for transfers between devices, return_all_the_signs(): load = lax.psum(load, b)  335 us
    scatter-add x1, other arithmetic, triplet_gradients(): gradient = gradient.at[triple[1]].add(-pull_term)  16.7 us
    scatter-add x1, other arithmetic, triplet_gradients(): gradient = gradient.at[triple[2]].add(push_term)  16.6 us
    scatter-add x1, other arithmetic, triplet_gradients(): gradient = gradient.at[triple[0]].add(pull_term - push_term)  15.1 us
    scatter-add x1, other arithmetic, local(): row_total = gradient[:shard_rows].at[served_index.reshape(-1)].add(return...  13.4 us
    all_to_all x1, waiting for transfers between devices, local(): lax.all_to_all(served, 'group', split_axis=0, concat_axis=0, tiled=True)  12.3 us
    all_to_all x1, waiting for transfers between devices, local(): lax.all_to_all(remote_grad, 'group', split_axis=0, concat_axis=0, tiled=T...  10.4 us
  transfers between devices with their start and end apart: 5, of which 5 were waited for; matrix products, arithmetic and copies ran while one was open for 1% of the time, Pallas kernels for 0%

profile of v1, /device:TPU:1, one launch (start us, length us, event | category | flops | bytes accessed | tf_op | source)
XLA Modules:
  0.0 509.9 jit_solution(5046727615045118211)
XLA Ops:
  7.2 0.0 copy-start
  7.2 7.7 %all-to-all-start = ((s32[16,1,128]{2,1,0:T(1,128)}), s32[16,1,128]{2,1,0:T(1,128)S(1)}, u32[]{:S(2)}, u32[]{:S(2)}) async-start(s32[16,1,128]{2,1,0:T(1,128)} %bitcast.29), calls=%async_computation | async-start | bytes 16384 | tf_op jit(solution)/shard_map/all_to_all | solution.py:48
  14.9 0.0 copy-done
  14.9 1.7 convolution_convert_fusion.1
  16.6 4.6 all-to-all-done
  21.3 9.1 %gather_fusion = bf16[2048,256]{1,0:T(8,128)(2,1)} fusion(bf16[1280,256]{1,0:T(8,128)(2,1)S(1)} %convolution_convert_fusion.1, s32[2048]{0:T(1024)S(1)} %broadcast_clamp_fusion.3), kind=kCustom, calls=%fused_computation | custom fusion | bytes 2105344 | tf_op jit(solution)/shard_map/gather | solution.py:50
  30.3 0.0 copy-start.1
  30.3 4.5 all-to-all-start.1
  34.8 0.0 copy-done.1
  34.9 12.3 %all-to-all-done.1 = bf16[16,128,256]{2,1,0:T(8,128)(2,1)} async-done(((bf16[16,128,256]{2,1,0:T(8,128)(2,1)}), bf16[16,128,256]{2,1,0:T(8,128)(2,1)}, u32[]{:S(2)}, u32[]{:S(2)}) %all-to-all-start.1) | async-done | bytes 1048608 | tf_op jit(solution)/shard_map/all_to_all | solution.py:51
  47.2 2.5 pad_maximum_fusion
  49.7 8.3 %gather_fusion.1 = bf16[2048,256]{1,0:T(8,128)(2,1)S(1)} fusion(bf16[3328,256]{1,0:T(8,128)(2,1)} %pad_maximum_fusion, s32[2048]{0:T(1024)S(1)} %broadcast_clamp_fusion.2), kind=kCustom, calls=%fused_computation.1 | custom fusion | bytes 2105344 | tf_op jit(solution)/shard_map/gather | solution.py:21
  58.0 10.1 %gather_fusion.3 = bf16[2048,256]{1,0:T(8,128)(2,1)} fusion(bf16[3328,256]{1,0:T(8,128)(2,1)} %pad_maximum_fusion, s32[2048]{0:T(1024)S(1)} %broadcast_clamp_fusion), kind=kCustom, calls=%fused_computation.3 | custom fusion | bytes 2105344 | tf_op jit(solution)/shard_map/gather | solution.py:23
  68.1 10.1 %gather_fusion.2 = bf16[2048,256]{1,0:T(8,128)(2,1)} fusion(bf16[3328,256]{1,0:T(8,128)(2,1)} %pad_maximum_fusion, s32[2048]{0:T(1024)S(1)} %broadcast_clamp_fusion.1), kind=kCustom, calls=%fused_computation.2 | custom fusion | bytes 2105344 | tf_op jit(solution)/shard_map/gather | solution.py:22
  78.2 0.0 copy-start.2
  78.2 2.5 multiply_reduce_fusion.1
  80.7 0.0 copy-done.2
  80.8 15.1 %scatter_custom_fusion = f32[3328,256]{1,0:T(8,128)} fusion(s32[2048]{0:T(1024)S(1)} %bitcast.28, bf16[2048,256]{1,0:T(8,128)(2,1)} %gather_fusion.3, bf16[2048,256]{1,0:T(8,128)(2,1)S(1)} %gather_fusion.1, bf16[2048,256]{1,0:T(8,128)(2,1)} %gather_fusion.2, f32[]{:T(128)} %constant.8.clone.1, f32[2048]{0:T(1024)S(1)} %get-tuple-element.8, ...), kind=kCustom, calls=%fused_computation.17 | custom fusion | flops 4718592 | bytes 6569988 | tf_op jit(solution)/shard_map/scatter-add | solution.py:34
  95.9 16.7 %scatter_custom_fusion.1 = f32[3328,256]{1,0:T(8,128)} fusion(f32[3328,256]{1,0:T(8,128)} %scatter_custom_fusion, s32[2048]{0:T(1024)S(1)} %bitcast.26, bf16[2048,256]{1,0:T(8,128)(2,1)} %gather_fusion.2, bf16[2048,256]{1,0:T(8,128)(2,1)S(1)} %gather_fusion.1, f32[2048]{0:T(1024)S(1)} %get-tuple-element.7), kind=kCustom, calls=%fused_computation.15 | custom fusion | flops 3145728 | bytes 5513216 | tf_op jit(solution)/shard_map/scatter-add | solution.py:35
  112.6 16.6 %scatter_custom_fusion.2 = f32[3328,256]{1,0:T(8,128)} fusion(f32[3328,256]{1,0:T(8,128)} %scatter_custom_fusion.1, s32[2048]{0:T(1024)S(1)} %bitcast.24, bf16[2048,256]{1,0:T(8,128)(2,1)} %gather_fusion.3, bf16[2048,256]{1,0:T(8,128)(2,1)S(1)} %gather_fusion.1, f32[2048]{0:T(1024)S(1)} %get-tuple-element.8), kind=kCustom, calls=%fused_computation.23 | custom fusion | flops 2621440 | bytes 5513216 | tf_op jit(solution)/shard_map/scatter-add | solution.py:36
  129.2 2.7 slice.38
  131.9 4.4 all-to-all-start.2
  136.2 0.0 all-reduce.3.cloned.1.call-start
  136.3 1.4 slice.32
  137.7 10.4 %all-to-all-done.2 = bf16[16,128,256]{2,1,0:T(8,128)(2,1)} async-done(((bf16[16,128,256]{2,1,0:T(8,128)(2,1)}), bf16[16,128,256]{2,1,0:T(8,128)(2,1)}, u32[]{:S(2)}, u32[]{:S(2)}) %all-to-all-start.2) | async-done | bytes 1048608 | tf_op jit(solution)/shard_map/all_to_all | solution.py:55
  148.1 13.4 %scatter_custom_fusion.3 = f32[1280,256]{1,0:T(8,128)S(1)} fusion(f32[1280,256]{1,0:T(8,128)S(1)} %slice.32, s32[2048]{0:T(1024)S(1)} %bitcast.22, bf16[2048,256]{1,0:T(8,128)(2,1)} %bitcast.12), kind=kCustom, calls=%fused_computation.13 | custom fusion | flops 1048576 | bytes 2359296 | tf_op jit(solution)/shard_map/scatter-add | solution.py:59
  161.6 1.6 fusion.18
  163.2 0.0 all-reduce.3.cloned.1.call-update
  163.2 0.0 all-reduce.5.cloned.1.call-start
  163.2 124.8 %all-reduce.3.cloned.1.call-done = f32[256,768]{1,0:T(8,128)} async-done(((f32[256,768]{1,0:T(8,128)}), f32[256,768]{1,0:T(8,128)}) %all-reduce.3.cloned.1.call-update) | async-done | bytes 786448 | tf_op jit(solution)/shard_map/psum | solution.py:16
  288.0 0.0 all-reduce.5.cloned.1.call-update
  288.1 2.9 convolution_convert_fusion
  291.0 210.0 %all-reduce.5.cloned.1.call-done = f32[256,768]{1,0:T(8,128)} async-done(((f32[256,768]{1,0:T(8,128)}), f32[256,768]{1,0:T(8,128)}) %all-reduce.5.cloned.1.call-update) | async-done | bytes 786448 | tf_op jit(solution)/shard_map/psum | solution.py:16
  501.0 2.1 broadcast_multiply_fusion
  (7 shorter events, 0.1 us)
Async XLA Ops:
  7.2 7.8 %copy-start = (bf16[1280,768]{1,0:T(8,128)(2,1)S(1)}, bf16[1280,768]{1,0:T(8,128)(2,1)}, u32[]{:S(2)}) copy-start(bf16[1280,768]{1,0:T(8,128)(2,1)} %param.5) | copy-start | bytes 5898244
  7.2 14.1 %all-to-all-start = ((s32[16,1,128]{2,1,0:T(1,128)}), s32[16,1,128]{2,1,0:T(1,128)S(1)}, u32[]{:S(2)}, u32[]{:S(2)}) async-start(s32[16,1,128]{2,1,0:T(1,128)} %bitcast.29), calls=%async_computation | async-start | bytes 16384 | tf_op jit(solution)/shard_map/all_to_all | solution.py:48
  30.3 4.5 copy-start.1
  30.3 16.8 %all-to-all-start.1 = ((bf16[16,128,256]{2,1,0:T(8,128)(2,1)}), bf16[16,128,256]{2,1,0:T(8,128)(2,1)}, u32[]{:S(2)}, u32[]{:S(2)}) async-start(bf16[16,128,256]{2,1,0:T(8,128)(2,1)} %bitcast.20), calls=%async_computation.1 | async-start | bytes 2097152 | tf_op jit(solution)/shard_map/all_to_all | solution.py:51
  78.2 2.5 copy-start.2
  131.9 16.3 %all-to-all-start.2 = ((bf16[16,128,256]{2,1,0:T(8,128)(2,1)}), bf16[16,128,256]{2,1,0:T(8,128)(2,1)}, u32[]{:S(2)}, u32[]{:S(2)}) async-start(bf16[16,128,256]{2,1,0:T(8,128)(2,1)} %bitcast.10), calls=%async_computation.2 | async-start | bytes 2097152 | tf_op jit(solution)/shard_map/all_to_all | solution.py:55
  136.2 151.8 %all-reduce.3.cloned.1.call-start = ((), (), s32[]{:S(2)}) async-start(), calls=%async_computation.3 | async-start | bytes 1572864 | tf_op jit(solution)/shard_map/psum | solution.py:16
  163.2 337.8 %all-reduce.5.cloned.1.call-start = ((), (), s32[]{:S(2)}) async-start(), calls=%async_computation.4 | async-start | bytes 1572864 | tf_op jit(solution)/shard_map/psum | solution.py:16
Sparse Core Ops, SparseCore 0:
  163.3 124.6 all-reduce.2
  290.5 210.4 all-reduce.4
